TPU v7x, 128 devices: a whole 4x4x4 slice. The times are simulated.
128 devices in a mesh: agent: 8 (over z, core), chan: 8 (over y, x_hi), batch: 2 (over x_lo).
Axes of the slice: x: 4 (x_hi: 2, x_lo: 2; x = x_hi * 2 + x_lo), y: 4, z: 4, core: 2. Of those that a mesh axis runs over, the one named last changes fastest.
Arguments:
- features: bfloat16 [256, 16, 16384], P(None, None, ('agent', 'chan', 'batch')), may hold values from -6 to 6
- norm_gain: float32 [256], replicated, may hold values from 0.1 to 1.9
- tok_in: bfloat16 [16384, 2048], P('agent'), may hold values from -0.046875 to 0.046875
- tok_out: bfloat16 [2048, 16384], P(None, 'agent'), may hold values from -0.125 to 0.125
- mix_gain: float32 [256], replicated, may hold values from 0.1 to 1.9
- chan_in: bfloat16 [256, 1024], replicated, may hold values from -0.375 to 0.375
- chan_out: bfloat16 [1024, 256], replicated, may hold values from -0.1875 to 0.1875
- head: bfloat16 [256, 8], replicated, may hold values from -8 to 8
- actions: int32 [16, 16384], P(None, ('agent', 'chan', 'batch')), may hold values from 0 to 7
- order: int32 [16384], P(('agent', 'chan', 'batch')), may hold values from 0 to 16383, as said below
Outputs:
- input_grad: float32 [256, 16, 16384], P(None, None, ('agent', 'chan', 'batch'))
- head_grad: float32 [256, 8], replicated
Inputs may be any that keep to these rules, and one draw needn't show every extreme that they name: order maps each aligned block of 128 agents one to one onto the same block.
All inputs are finite; a program needn't handle non-finite values.
Results may differ from a plain program's by a relative error of at most 0.025.
Values may be sent and summed in bfloat16 or wider, within the bound.
A program may use at most 128 MiB of HBM per device.

v0:
```python
import jax
import jax.numpy as jnp
from jax import lax
from jax.sharding import PartitionSpec as P

A = 16384
GELU_K = 0.7978845608028654
GELU_C = 0.044715
EPS = 1e-05


def gelu_value(v):
    return 0.5 * v * (1.0 + jnp.tanh(GELU_K * (v + GELU_C * v * v * v)))


def gelu_slope(v):
    inner = jnp.tanh(GELU_K * (v + GELU_C * v * v * v))
    return 0.5 * (1.0 + inner) + 0.5 * v * (1.0 - inner * inner) * GELU_K * (
        1.0 + 3.0 * GELU_C * v * v
    )


def shaped_gain(gain, field):
    return gain.reshape((gain.shape[0],) + (1,) * (field.ndim - 1))


def norm_forward(field, gain):
    center = jnp.mean(field, axis=0, keepdims=True)
    spread = jnp.mean(jnp.square(field - center), axis=0, keepdims=True)
    scale = lax.rsqrt(spread + EPS)
    unit = (field - center) * scale
    return (unit * shaped_gain(gain, field), unit, scale)


def norm_backward(upstream, gain, unit, scale):
    weighted = upstream * shaped_gain(gain, upstream)
    return scale * (
        weighted
        - jnp.mean(weighted, axis=0, keepdims=True)
        - unit * jnp.mean(weighted * unit, axis=0, keepdims=True)
    )


def to_tokens(field):
    return lax.all_to_all(field, ("chan", "batch"), split_axis=0, concat_axis=2, tiled=True)


def to_channels(field):
    return lax.all_to_all(field, ("chan", "batch"), split_axis=2, concat_axis=0, tiled=True)


def project(weight, hidden_dim, rows):
    agent_dim = 1 - hidden_dim
    partial_sum = lax.dot_general(
        weight, rows, (((agent_dim,), (1,)), ((), ())), preferred_element_type=jnp.float32
    )
    return lax.psum(partial_sum, "agent")


def expand(spread, weight, hidden_dim):
    return lax.dot_general(
        spread, weight, (((0,), (hidden_dim,)), ((), ())), preferred_element_type=jnp.float32
    )


def shards(features, norm_gain, tok_in, tok_out, mix_gain, chan_in, chan_out, head, actions, order):
    wide = features.astype(jnp.float32)
    chans, samples, local = wide.shape
    normed_in, unit_in, scale_in = norm_forward(wide, norm_gain)
    spread_in = to_tokens(normed_in.astype(jnp.bfloat16))
    token_chans, _, agents = spread_in.shape
    token_rows = spread_in.reshape(token_chans * samples, agents)
    hidden_pre = project(tok_in, 1, token_rows)
    hidden_act = gelu_value(hidden_pre).astype(jnp.bfloat16)
    mixed = (
        expand(hidden_act, tok_out, 0).astype(jnp.bfloat16).reshape(token_chans, samples, agents)
    )
    mixed_back = to_channels(mixed)
    first = wide + mixed_back.astype(jnp.float32)
    normed_mid, unit_mid, scale_mid = norm_forward(first, mix_gain)
    flat_mid = normed_mid.astype(jnp.bfloat16).reshape(chans, samples * local)
    inner_pre = lax.dot_general(
        chan_in, flat_mid, (((0,), (0,)), ((), ())), preferred_element_type=jnp.float32
    )
    inner = gelu_value(inner_pre).astype(jnp.bfloat16)
    outer = lax.dot_general(
        chan_out, inner, (((0,), (0,)), ((), ())), preferred_element_type=jnp.float32
    )
    second = (first.reshape(chans, samples * local) + outer).astype(jnp.bfloat16)
    logits = lax.dot_general(
        head, second, (((0,), (0,)), ((), ())), preferred_element_type=jnp.float32
    )
    target = jnp.take_along_axis(actions, (order % local)[None, :], axis=1).reshape(
        1, samples * local
    )
    phases = lax.broadcasted_iota(jnp.int32, logits.shape, 0)
    picked = (phases == target).astype(jnp.float32)
    top = jnp.max(logits, axis=0, keepdims=True)
    exps = jnp.exp(logits - top)
    probs = exps / jnp.sum(exps, axis=0, keepdims=True)
    slope = (probs - picked).astype(jnp.bfloat16)
    head_part = lax.dot_general(
        second, slope, (((1,), (1,)), ((), ())), preferred_element_type=jnp.float32
    )
    head_total = lax.psum(head_part, ("agent", "chan", "batch"))
    head_grad = head_total * (1.0 / (samples * A))
    back_second = lax.dot_general(
        head, slope, (((1,), (0,)), ((), ())), preferred_element_type=jnp.float32
    )
    back_low = back_second.astype(jnp.bfloat16)
    back_inner = lax.dot_general(
        chan_out, back_low, (((1,), (0,)), ((), ())), preferred_element_type=jnp.float32
    )
    back_inner_pre = (back_inner * gelu_slope(inner_pre)).astype(jnp.bfloat16)
    back_mid = lax.dot_general(
        chan_in, back_inner_pre, (((1,), (0,)), ((), ())), preferred_element_type=jnp.float32
    )
    back_first = back_second.reshape(chans, samples, local) + norm_backward(
        back_mid.reshape(chans, samples, local), mix_gain, unit_mid, scale_mid
    )
    back_tokens = to_tokens(back_first.astype(jnp.bfloat16))
    back_rows = back_tokens.reshape(token_chans * samples, agents)
    back_hidden = project(tok_out, 0, back_rows)
    back_hidden_pre = (back_hidden * gelu_slope(hidden_pre)).astype(jnp.bfloat16)
    back_spread = (
        expand(back_hidden_pre, tok_in, 1)
        .astype(jnp.bfloat16)
        .reshape(token_chans, samples, agents)
    )
    back_norm = to_channels(back_spread)
    input_grad = back_first + norm_backward(
        back_norm.astype(jnp.float32), norm_gain, unit_in, scale_in
    )
    return (input_grad, head_grad)


def solution(mesh):
    in_specs = (
        P(None, None, ("agent", "chan", "batch")),
        P(),
        P("agent", None),
        P(None, "agent"),
        P(),
        P(),
        P(),
        P(),
        P(None, ("agent", "chan", "batch")),
        P(("agent", "chan", "batch")),
    )
    out_specs = (P(None, None, ("agent", "chan", "batch")), P())
    return jax.shard_map(shards, mesh=mesh, in_specs=in_specs, out_specs=out_specs, check_vma=False)
```

profile of v0, /device:TPU:1, one launch (start us, length us, event | category | flops | bytes accessed | tf_op | source)
XLA Modules:
  0.0 469.4 jit_solution(13224073951282337597)
XLA Ops:
  7.2 1.6 convert_reduce_fusion
  8.9 1.5 fusion.21
  10.4 0.4 fusion.16
  10.8 23.5 %all_to_all.48 = bf16[256,16,128]{2,1,0:T(8,128)(2,1)S(1)} all-to-all(bf16[256,16,128]{2,1,0:T(8,128)(2,1)S(1)} %fusion.16), channel_id=1, replica_groups=mesh['agent'=8,'chan'=8,'batch'=2] {'chan','batch'}, dimensions={0} | all-to-all | bytes 2097152 | tf_op jit(solution)/shard_map/all_to_all | solution.py:45
  34.3 0.7 copy.56
  35.0 7.0 %convolution_bitcast_fusion.1 = f32[2048,256]{0,1:T(8,128)} fusion(bf16[2048,2048]{1,0:T(8,128)(2,1)} %param.12, bf16[32,8,16,128]{3,2,1,0:T(8,128)(2,1)S(1)} %bitcast.134), kind=kOutput, calls=%fused_computation.23 | convolution fusion | flops 2147483648 | bytes 11534336 | tf_op jit(solution)/shard_map/dot_general | solution.py:54
  42.1 64.0 %all-reduce.3.cloned.1.call-done = f32[2048,256]{0,1:T(8,128)} async-done(((f32[2048,256]{0,1:T(8,128)}), f32[2048,256]{0,1:T(8,128)}) %all-reduce.3.cloned.1.call-update) | async-done | bytes 2097168 | tf_op jit(solution)/shard_map/psum | solution.py:57
  106.1 6.6 %convolution_convert_fusion.1 = bf16[256,2048]{1,0:T(8,128)(2,1)S(1)} fusion(bf16[2048,2048]{1,0:T(8,128)(2,1)} %param.13, f32[2048,256]{0,1:T(8,128)} %all-reduce.3.cloned.1.call-done), kind=kOutput, calls=%fused_computation.27 | convolution fusion | flops 2152726528 | bytes 11534336 | tf_op jit(solution)/shard_map/dot_general | solution.py:61
  112.6 8.5 %copy.57 = bf16[16,16,2048]{1,0,2:T(8,128)(2,1)} copy(bf16[16,16,2048]{2,1,0:T(8,128)(2,1)S(1)} %bitcast.133) | data formatting | bytes 2097152 | tf_op jit(solution)/shard_map/reshape | solution.py:76
  121.1 11.2 %reshape.152 = bf16[16,2,16384]{2,1,0:T(2,128)(2,1)} reshape(bf16[2048,16,16]{2,1,0:T(8,128)(2,1)} %bitcast.124) | data formatting | bytes 2097152
  132.4 6.7 %all-to-all-start.1 = ((bf16[16,2,16384]{2,1,0:T(2,128)(2,1)}), bf16[16,2,16384]{2,1,0:T(2,128)(2,1)S(1)}, u32[]{:S(2)}, u32[]{:S(2)}) async-start(bf16[16,2,16384]{2,1,0:T(2,128)(2,1)} %reshape.152), calls=%async_computation.1 | async-start | bytes 2097152 | tf_op jit(solution)/shard_map/all_to_all | solution.py:49
  139.0 0.5 all-reduce.5.cloned.1.call-start
  139.7 0.6 gather_fusion
  140.5 13.1 %all-to-all-done.1 = bf16[16,2,16384]{2,1,0:T(2,128)(2,1)S(1)} async-done(((bf16[16,2,16384]{2,1,0:T(2,128)(2,1)}), bf16[16,2,16384]{2,1,0:T(2,128)(2,1)S(1)}, u32[]{:S(2)}, u32[]{:S(2)}) %all-to-all-start.1) | async-done | bytes 1048608 | tf_op jit(solution)/shard_map/all_to_all | solution.py:49
  153.6 7.5 %reshape.153 = bf16[2048,16,16]{2,1,0:T(8,128)(2,1)} reshape(bf16[16,2,16384]{2,1,0:T(2,128)(2,1)S(1)} %all-to-all-done.1) | data formatting | bytes 2097152
  161.1 10.9 %convert_bitcast_fusion = f32[16,16,16,128]{2,1,3,0:T(8,128)} fusion(bf16[16,16,16,128]{1,0,3,2:T(8,128)(2,1)} %bitcast.123), kind=kLoop, calls=%fused_computation.1 | loop fusion | flops 524288 | bytes 3145728 | tf_op jit(solution)/shard_map/convert_element_type | solution.py:79
  172.0 11.4 %copy.58 = f32[16,16,16,128]{3,2,1,0:T(8,128)} copy(f32[16,16,16,128]{2,1,3,0:T(8,128)} %convert_bitcast_fusion) | data formatting | bytes 4194304 | tf_op jit(solution)/shard_map/convert_element_type | solution.py:79
  183.4 2.2 fusion.76
  185.6 1.8 copy.59
  187.7 0.4 copy-done.13
  188.1 0.4 multiply_convert_fusion.8
  188.5 1.3 fusion.34
  190.1 3.0 fusion.10
  193.2 0.4 fusion.77
  193.6 0.6 copy-done.8
  194.2 1.8 fusion.71
  196.0 9.5 %fusion.29 = (f32[2048]{0:T(1024)S(1)}, f32[2048,256]{1,0:T(8,128)}) fusion(f32[256]{0:T(256)S(1)} %copy-done.13, bf16[256,1024]{1,0:T(8,128)(2,1)S(1)} %copy-done, f32[2048,1024]{1,0:T(8,128)} %copy-done.6, bf16[1024,256]{1,0:T(8,128)(2,1)S(1)} %copy-done.15, f32[2048,256]{1,0:T(8,128)} %fusion.71), kind=kOutput, calls=%fused_computation.48 | convolution fusion | flops 2188376064 | bytes 13640704 | tf_op jit(solution)/shard_map/dot_general | solution.py:115
  205.5 3.1 copy.62
  208.6 3.2 copy.63
  211.8 2.1 multiply_reduce_fusion.1
  214.0 0.6 copy-done.7
  214.7 2.1 fusion.75
  216.7 17.1 %all_to_all.49 = bf16[256,16,128]{2,1,0:T(8,128)(2,1)S(1)} all-to-all(bf16[256,16,128]{2,1,0:T(8,128)(2,1)S(1)} %get-tuple-element.2), channel_id=1, replica_groups=mesh['agent'=8,'chan'=8,'batch'=2] {'chan','batch'}, dimensions={0} | all-to-all | bytes 2097152 | tf_op jit(solution)/shard_map/all_to_all | solution.py:45
  233.8 0.7 copy.64
  234.5 7.0 %convolution_bitcast_fusion = f32[2048,256]{0,1:T(8,128)} fusion(bf16[2048,2048]{1,0:T(8,128)(2,1)} %param.13, bf16[32,8,16,128]{3,2,1,0:T(8,128)(2,1)S(1)} %bitcast.135), kind=kOutput, calls=%fused_computation.22 | convolution fusion | flops 2147483648 | bytes 11534336 | tf_op jit(solution)/shard_map/dot_general | solution.py:54
  241.5 70.8 %all-reduce.5.cloned.1.call-done = f32[2048,256]{0,1:T(8,128)} async-done(((f32[2048,256]{0,1:T(8,128)}), f32[2048,256]{0,1:T(8,128)}) %all-reduce.5.cloned.1.call-update) | async-done | bytes 2097168 | tf_op jit(solution)/shard_map/psum | solution.py:57
  312.3 7.8 %convolution_convert_fusion = bf16[256,2048]{1,0:T(8,128)(2,1)S(1)} fusion(bf16[2048,2048]{1,0:T(8,128)(2,1)} %param.12, f32[2048,256]{0,1:T(8,128)} %all-reduce.5.cloned.1.call-done, f32[2048,256]{0,1:T(8,128)} %all-reduce.3.cloned.1.call-done), kind=kOutput, calls=%fused_computation.26 | convolution fusion | flops 2157969408 | bytes 13631488 | tf_op jit(solution)/shard_map/dot_general | solution.py:61
  320.1 8.5 %copy.65 = bf16[16,16,2048]{1,0,2:T(8,128)(2,1)} copy(bf16[16,16,2048]{2,1,0:T(8,128)(2,1)S(1)} %bitcast.132) | data formatting | bytes 2097152 | tf_op jit(solution)/shard_map/reshape | solution.py:128
  328.6 11.2 %reshape.154 = bf16[16,2,16384]{2,1,0:T(2,128)(2,1)} reshape(bf16[2048,16,16]{2,1,0:T(8,128)(2,1)} %bitcast.125) | data formatting | bytes 2097152
  339.9 6.7 %all-to-all-start.3 = ((bf16[16,2,16384]{2,1,0:T(2,128)(2,1)}), bf16[16,2,16384]{2,1,0:T(2,128)(2,1)S(1)}, u32[]{:S(2)}, u32[]{:S(2)}) async-start(bf16[16,2,16384]{2,1,0:T(2,128)(2,1)} %reshape.154), calls=%async_computation.3 | async-start | bytes 2097152 | tf_op jit(solution)/shard_map/all_to_all | solution.py:49
  346.9 73.3 %psum.23 = f32[256,8]{0,1:T(8,128)S(1)} all-reduce(f32[256,8]{0,1:T(8,128)S(1)} %fusion.69), channel_id=1, replica_groups=mesh['agent'=8,'chan'=8,'batch'=2] {'agent','chan','batch'}, use_global_device_ids=true, to_apply=%region_12.13 | all-reduce | flops 2048 | bytes 16384 | tf_op jit(solution)/shard_map/psum | solution.py:105
  420.2 0.6 broadcast_multiply_fusion
  420.8 7.5 %reshape.155 = bf16[2048,16,16]{2,1,0:T(8,128)(2,1)} reshape(bf16[16,2,16384]{2,1,0:T(2,128)(2,1)S(1)} %all-to-all-done.3) | data formatting | bytes 2097152
  428.3 10.9 %convert_bitcast_fusion.1 = f32[16,16,16,128]{2,1,3,0:T(8,128)} fusion(bf16[2048,16,16]{2,1,0:T(8,128)(2,1)} %reshape.155), kind=kLoop, calls=%fused_computation.2 | loop fusion | flops 524288 | bytes 3145728 | tf_op jit(solution)/shard_map/convert_element_type | solution.py:132
  439.2 5.7 %multiply_reduce_fusion = f32[16,128]{0,1:T(8,128)S(1)} fusion(f32[16,16]{1,0:T(8,128)S(1)} %mul.242, bf16[16,16,16,128]{1,0,3,2:T(8,128)(2,1)} %bitcast.122), kind=kLoop, calls=%fused_computation.3 | loop fusion | flops 1570816 | bytes 1057792 | tf_op jit(solution)/shard_map/reduce_sum | solution.py:39
  445.0 11.5 %copy.66 = f32[16,16,16,128]{3,2,1,0:T(8,128)} copy(f32[16,16,16,128]{2,1,3,0:T(8,128)} %convert_bitcast_fusion.1) | data formatting | bytes 4194304 | tf_op jit(solution)/shard_map/convert_element_type | solution.py:132
  456.5 2.2 fusion.17
  458.7 3.6 fusion.20
  (52 shorter events, 1.5 us)
Async XLA Ops:
  7.2 181.3 %copy-start = (bf16[256,1024]{1,0:T(8,128)(2,1)S(1)}, bf16[256,1024]{1,0:T(8,128)(2,1)}, u32[]{:S(2)}) copy-start(bf16[256,1024]{1,0:T(8,128)(2,1)} %param.15) | copy-start | bytes 1572868
  7.2 3.2 copy-start.2
  7.2 3.2 copy-start.12
  7.2 98.9 %all-reduce.3.cloned.1.call-start = ((), (), s32[]{:S(2)}) async-start(), calls=%async_computation.4 | async-start | bytes 4194304 | tf_op jit(solution)/shard_map/psum | solution.py:57
  132.4 7.2 %copy-start.14 = (s32[16,128]{1,0:T(8,128)S(1)}, s32[16,128]{1,0:T(8,128)}, u32[]{:S(2)}) copy-start(s32[16,128]{1,0:T(8,128)} %param.18) | copy-start | bytes 24580
  132.4 7.3 %copy-start.16 = (s32[128]{0:T(128)S(1)}, s32[128]{0:T(128)}, u32[]{:S(2)}) copy-start(s32[128]{0:T(128)} %param.19) | copy-start | bytes 1540
  132.4 21.2 %all-to-all-start.1 = ((bf16[16,2,16384]{2,1,0:T(2,128)(2,1)}), bf16[16,2,16384]{2,1,0:T(2,128)(2,1)S(1)}, u32[]{:S(2)}, u32[]{:S(2)}) async-start(bf16[16,2,16384]{2,1,0:T(2,128)(2,1)} %reshape.152), calls=%async_computation.1 | async-start | bytes 2097152 | tf_op jit(solution)/shard_map/all_to_all | solution.py:49
  139.0 173.2 %all-reduce.5.cloned.1.call-start = ((), (), s32[]{:S(2)}) async-start(), calls=%async_computation.5 | async-start | bytes 4194304 | tf_op jit(solution)/shard_map/psum | solution.py:57
  187.4 0.7 copy-start.13
  188.4 1.6 copy-start.10
  188.5 1.7 copy-start.15
  189.8 3.3 copy-start.6
  190.1 3.0 copy-start.11
  193.2 1.0 copy-start.8
  211.8 2.2 copy-start.4
  211.8 2.8 copy-start.7
  339.9 6.7 %copy-start.9 = (bf16[256,2048]{0,1:T(8,128)(2,1)S(1)}, bf16[256,2048]{0,1:T(8,128)(2,1)}, u32[]{:S(2)}) copy-start(bf16[256,2048]{0,1:T(8,128)(2,1)} %copy-done.8) | copy-start | bytes 3145732
  339.9 80.9 %all-to-all-start.3 = ((bf16[16,2,16384]{2,1,0:T(2,128)(2,1)}), bf16[16,2,16384]{2,1,0:T(2,128)(2,1)S(1)}, u32[]{:S(2)}, u32[]{:S(2)}) async-start(bf16[16,2,16384]{2,1,0:T(2,128)(2,1)} %reshape.154), calls=%async_computation.3 | async-start | bytes 2097152 | tf_op jit(solution)/shard_map/all_to_all | solution.py:49
  444.9 11.5 %copy-start.3 = (bf16[256,16,128]{2,1,0:T(8,128)(2,1)S(1)}, bf16[256,16,128]{2,1,0:T(8,128)(2,1)}, u32[]{:S(2)}) copy-start(bf16[256,16,128]{2,1,0:T(8,128)(2,1)} %param.10) | copy-start | bytes 3145732
  456.5 2.2 copy-start.5
  458.7 3.6 copy-start.1
Sparse Core Ops, SparseCore 0:
  42.2 63.8 all-reduce.2
  241.7 70.5 all-reduce.4
where the time goes:
time: 477 us; the launch traced here: 469 us
  waiting for transfers between devices  148 us (31%)
  blocking collectives  114 us (24%)
  local copies, waits for them, and re-layouts  89.9 us (19%)
  matrix products  44.8 us (9%)
  other arithmetic  44.6 us (9%)
  between operations  14.6 us (3%)
  starting transfers between devices  13.9 us (3%)
    psum x2, waiting for transfers between devices, project(): return lax.psum(partial_sum, 'agent')  135 us
    psum x1, blocking collectives, shards(): head_total = lax.psum(head_part, ('agent', 'chan', 'batch'))  73.3 us
    all_to_all x2, blocking collectives, to_tokens(): lax.all_to_all(field, ('chan', 'batch'), split_axis=0, concat_axis=2, til...  40.6 us
    unnamed x39, local copies, waits for them, and re-layouts  39.6 us
    dot_general x2, matrix products, expand(): lax.dot_general(spread, weight, (((0,), (hidden_dim,)), ((), ())), prefer...  14.4 us
    dot_general x2, matrix products, project(): lax.dot_general(weight, rows, (((agent_dim,), (1,)), ((), ())), preferred...  14.1 us
    all_to_all x2, starting transfers between devices, to_channels(): lax.all_to_all(field, ('chan', 'batch'), split_axis=2, concat_axis=0, til...  13.3 us
    all_to_all x2, waiting for transfers between devices, to_channels(): lax.all_to_all(field, ('chan', 'batch'), split_axis=2, concat_axis=0, til...  13.1 us
  transfers between devices with their start and end apart: 4, of which 3 were waited for; matrix products, arithmetic and copies ran while one was open for 0% of the time, Pallas kernels for 0%

commit v1 on v0

--- a/solution.py
+++ b/solution.py
@@ -102,7 +102,7 @@
     head_part = lax.dot_general(
         second, slope, (((1,), (1,)), ((), ())), preferred_element_type=jnp.float32
     )
-    head_total = lax.psum(head_part, ("agent", "chan", "batch"))
+    head_total = lax.psum(lax.psum(head_part, ("chan", "batch")), "agent")
     head_grad = head_total * (1.0 / (samples * A))
     back_second = lax.dot_general(
         head, slope, (((1,), (0,)), ((), ())), preferred_element_type=jnp.float32

time: 477 us -> 459 us (0.962); the launches traced: 469 us -> 457 us
  blocking collectives: 114 us -> 102 us
    psum x1 -> x2, blocking collectives: 73.3 us -> 61.4 us  [shards(): head_total = lax.psum(lax.psum(head_part, ('chan', 'batch')), 'agent')]
where the time goes in v1:
time: 459 us; the launch traced here: 457 us
  waiting for transfers between devices  148 us (32%)
  blocking collectives  102 us (22%)
  local copies, waits for them, and re-layouts  89.7 us (20%)
  matrix products  44.8 us (10%)
  other arithmetic  44.6 us (10%)
  between operations  14.3 us (3%)
  starting transfers between devices  13.6 us (3%)
    psum x2, waiting for transfers between devices, project(): return lax.psum(partial_sum, 'agent')  135 us
    psum x2, blocking collectives, shards(): head_total = lax.psum(lax.psum(head_part, ('chan', 'batch')), 'agent')  61.4 us
    all_to_all x2, blocking collectives, to_tokens(): lax.all_to_all(field, ('chan', 'batch'), split_axis=0, concat_axis=2, til...  40.6 us
    unnamed x39, local copies, waits for them, and re-layouts  39.7 us
    dot_general x2, matrix products, expand(): lax.dot_general(spread, weight, (((0,), (hidden_dim,)), ((), ())), prefer...  14.4 us
    dot_general x2, matrix products, project(): lax.dot_general(weight, rows, (((agent_dim,), (1,)), ((), ())), preferred...  14.1 us
    all_to_all x2, waiting for transfers between devices, to_channels(): lax.all_to_all(field, ('chan', 'batch'), split_axis=2, concat_axis=0, til...  13.4 us
    all_to_all x2, starting transfers between devices, to_channels(): lax.all_to_all(field, ('chan', 'batch'), split_axis=2, concat_axis=0, til...  13.3 us
  transfers between devices with their start and end apart: 4, of which 3 were waited for; matrix products, arithmetic and copies ran while one was open for 0% of the time, Pallas kernels for 0%

profile of v1, /device:TPU:1, one launch (start us, length us, event | category | flops | bytes accessed | tf_op | source)
XLA Modules:
  0.0 457.1 jit_solution(11943538280089385710)
XLA Ops:
  7.2 1.6 convert_reduce_fusion
  8.9 1.5 fusion.21
  10.4 0.4 fusion.16
  10.8 23.5 %all_to_all.48 = bf16[256,16,128]{2,1,0:T(8,128)(2,1)S(1)} all-to-all(bf16[256,16,128]{2,1,0:T(8,128)(2,1)S(1)} %fusion.16), channel_id=1, replica_groups=mesh['agent'=8,'chan'=8,'batch'=2] {'chan','batch'}, dimensions={0} | all-to-all | bytes 2097152 | tf_op jit(solution)/shard_map/all_to_all | solution.py:45
  34.3 0.7 copy.56
  35.0 7.0 %convolution_bitcast_fusion.1 = f32[2048,256]{0,1:T(8,128)} fusion(bf16[2048,2048]{1,0:T(8,128)(2,1)} %param.12, bf16[32,8,16,128]{3,2,1,0:T(8,128)(2,1)S(1)} %bitcast.134), kind=kOutput, calls=%fused_computation.23 | convolution fusion | flops 2147483648 | bytes 11534336 | tf_op jit(solution)/shard_map/dot_general | solution.py:54
  42.1 64.0 %all-reduce.3.cloned.1.call-done = f32[2048,256]{0,1:T(8,128)} async-done(((f32[2048,256]{0,1:T(8,128)}), f32[2048,256]{0,1:T(8,128)}) %all-reduce.3.cloned.1.call-update) | async-done | bytes 2097168 | tf_op jit(solution)/shard_map/psum | solution.py:57
  106.1 6.6 %convolution_convert_fusion.1 = bf16[256,2048]{1,0:T(8,128)(2,1)S(1)} fusion(bf16[2048,2048]{1,0:T(8,128)(2,1)} %param.13, f32[2048,256]{0,1:T(8,128)} %all-reduce.3.cloned.1.call-done), kind=kOutput, calls=%fused_computation.27 | convolution fusion | flops 2152726528 | bytes 11534336 | tf_op jit(solution)/shard_map/dot_general | solution.py:61
  112.6 8.5 %copy.57 = bf16[16,16,2048]{1,0,2:T(8,128)(2,1)} copy(bf16[16,16,2048]{2,1,0:T(8,128)(2,1)S(1)} %bitcast.133) | data formatting | bytes 2097152 | tf_op jit(solution)/shard_map/reshape | solution.py:76
  121.1 11.2 %reshape.152 = bf16[16,2,16384]{2,1,0:T(2,128)(2,1)} reshape(bf16[2048,16,16]{2,1,0:T(8,128)(2,1)} %bitcast.124) | data formatting | bytes 2097152
  132.4 6.7 %all-to-all-start.1 = ((bf16[16,2,16384]{2,1,0:T(2,128)(2,1)}), bf16[16,2,16384]{2,1,0:T(2,128)(2,1)S(1)}, u32[]{:S(2)}, u32[]{:S(2)}) async-start(bf16[16,2,16384]{2,1,0:T(2,128)(2,1)} %reshape.152), calls=%async_computation.1 | async-start | bytes 2097152 | tf_op jit(solution)/shard_map/all_to_all | solution.py:49
  139.4 0.6 gather_fusion
  140.2 13.4 %all-to-all-done.1 = bf16[16,2,16384]{2,1,0:T(2,128)(2,1)S(1)} async-done(((bf16[16,2,16384]{2,1,0:T(2,128)(2,1)}), bf16[16,2,16384]{2,1,0:T(2,128)(2,1)S(1)}, u32[]{:S(2)}, u32[]{:S(2)}) %all-to-all-start.1) | async-done | bytes 1048608 | tf_op jit(solution)/shard_map/all_to_all | solution.py:49
  153.6 7.5 %reshape.153 = bf16[2048,16,16]{2,1,0:T(8,128)(2,1)} reshape(bf16[16,2,16384]{2,1,0:T(2,128)(2,1)S(1)} %all-to-all-done.1) | data formatting | bytes 2097152
  161.1 10.9 %convert_bitcast_fusion = f32[16,16,16,128]{2,1,3,0:T(8,128)} fusion(bf16[16,16,16,128]{1,0,3,2:T(8,128)(2,1)} %bitcast.123), kind=kLoop, calls=%fused_computation.1 | loop fusion | flops 524288 | bytes 3145728 | tf_op jit(solution)/shard_map/convert_element_type | solution.py:79
  172.0 11.4 %copy.58 = f32[16,16,16,128]{3,2,1,0:T(8,128)} copy(f32[16,16,16,128]{2,1,3,0:T(8,128)} %convert_bitcast_fusion) | data formatting | bytes 4194304 | tf_op jit(solution)/shard_map/convert_element_type | solution.py:79
  183.4 2.2 fusion.76
  185.6 1.8 copy.59
  187.7 0.4 copy-done.13
  188.1 0.4 multiply_convert_fusion.8
  188.5 1.3 fusion.34
  190.1 3.0 fusion.10
  193.2 0.4 fusion.77
  193.6 0.6 copy-done.8
  194.2 1.8 fusion.71
  196.0 9.5 %fusion.29 = (f32[2048]{0:T(1024)S(1)}, f32[2048,256]{1,0:T(8,128)}) fusion(f32[256]{0:T(256)S(1)} %copy-done.13, bf16[256,1024]{1,0:T(8,128)(2,1)S(1)} %copy-done, f32[2048,1024]{1,0:T(8,128)} %copy-done.6, bf16[1024,256]{1,0:T(8,128)(2,1)S(1)} %copy-done.15, f32[2048,256]{1,0:T(8,128)} %fusion.71), kind=kOutput, calls=%fused_computation.48 | convolution fusion | flops 2188376064 | bytes 13640704 | tf_op jit(solution)/shard_map/dot_general | solution.py:115
  205.5 3.1 copy.62
  208.6 3.0 copy.63
  211.7 2.1 multiply_reduce_fusion.1
  213.9 0.6 copy-done.7
  214.5 2.1 fusion.75
  216.6 17.1 %all_to_all.49 = bf16[256,16,128]{2,1,0:T(8,128)(2,1)S(1)} all-to-all(bf16[256,16,128]{2,1,0:T(8,128)(2,1)S(1)} %get-tuple-element.2), channel_id=1, replica_groups=mesh['agent'=8,'chan'=8,'batch'=2] {'chan','batch'}, dimensions={0} | all-to-all | bytes 2097152 | tf_op jit(solution)/shard_map/all_to_all | solution.py:45
  233.7 0.7 copy.64
  234.3 7.0 %convolution_bitcast_fusion = f32[2048,256]{0,1:T(8,128)} fusion(bf16[2048,2048]{1,0:T(8,128)(2,1)} %param.13, bf16[32,8,16,128]{3,2,1,0:T(8,128)(2,1)S(1)} %bitcast.135), kind=kOutput, calls=%fused_computation.22 | convolution fusion | flops 2147483648 | bytes 11534336 | tf_op jit(solution)/shard_map/dot_general | solution.py:54
  241.4 70.7 %all-reduce.5.cloned.1.call-done = f32[2048,256]{0,1:T(8,128)} async-done(((f32[2048,256]{0,1:T(8,128)}), f32[2048,256]{0,1:T(8,128)}) %all-reduce.5.cloned.1.call-update) | async-done | bytes 2097168 | tf_op jit(solution)/shard_map/psum | solution.py:57
  312.1 7.8 %convolution_convert_fusion = bf16[256,2048]{1,0:T(8,128)(2,1)S(1)} fusion(bf16[2048,2048]{1,0:T(8,128)(2,1)} %param.12, f32[2048,256]{0,1:T(8,128)} %all-reduce.5.cloned.1.call-done, f32[2048,256]{0,1:T(8,128)} %all-reduce.3.cloned.1.call-done), kind=kOutput, calls=%fused_computation.26 | convolution fusion | flops 2157969408 | bytes 13631488 | tf_op jit(solution)/shard_map/dot_general | solution.py:61
  319.9 8.5 %copy.65 = bf16[16,16,2048]{1,0,2:T(8,128)(2,1)} copy(bf16[16,16,2048]{2,1,0:T(8,128)(2,1)S(1)} %bitcast.132) | data formatting | bytes 2097152 | tf_op jit(solution)/shard_map/reshape | solution.py:128
  328.4 11.2 %reshape.154 = bf16[16,2,16384]{2,1,0:T(2,128)(2,1)} reshape(bf16[2048,16,16]{2,1,0:T(8,128)(2,1)} %bitcast.125) | data formatting | bytes 2097152
  339.7 6.7 %all-to-all-start.3 = ((bf16[16,2,16384]{2,1,0:T(2,128)(2,1)}), bf16[16,2,16384]{2,1,0:T(2,128)(2,1)S(1)}, u32[]{:S(2)}, u32[]{:S(2)}) async-start(bf16[16,2,16384]{2,1,0:T(2,128)(2,1)} %reshape.154), calls=%async_computation.3 | async-start | bytes 2097152 | tf_op jit(solution)/shard_map/all_to_all | solution.py:49
  346.7 37.8 %psum.30 = f32[256,8]{0,1:T(8,128)S(1)} all-reduce(f32[256,8]{0,1:T(8,128)S(1)} %fusion.69), channel_id=1, replica_groups=mesh['agent'=8,'chan'=8,'batch'=2] {'chan','batch'}, use_global_device_ids=true, to_apply=%region_12.13 | all-reduce | flops 2048 | bytes 16384 | tf_op jit(solution)/shard_map/psum | solution.py:105
  384.4 23.6 %psum.31 = f32[256,8]{0,1:T(8,128)S(1)} all-reduce(f32[256,8]{0,1:T(8,128)S(1)} %psum.30), channel_id=1, replica_groups=mesh['agent'=8,'chan'=8,'batch'=2] {'agent'}, use_global_device_ids=true, to_apply=%region_13.14 | all-reduce | flops 2048 | bytes 16384 | tf_op jit(solution)/shard_map/psum | solution.py:105
  408.1 0.6 broadcast_multiply_fusion
  408.7 7.5 %reshape.155 = bf16[2048,16,16]{2,1,0:T(8,128)(2,1)} reshape(bf16[16,2,16384]{2,1,0:T(2,128)(2,1)S(1)} %all-to-all-done.3) | data formatting | bytes 2097152
  416.2 10.9 %convert_bitcast_fusion.1 = f32[16,16,16,128]{2,1,3,0:T(8,128)} fusion(bf16[2048,16,16]{2,1,0:T(8,128)(2,1)} %reshape.155), kind=kLoop, calls=%fused_computation.2 | loop fusion | flops 524288 | bytes 3145728 | tf_op jit(solution)/shard_map/convert_element_type | solution.py:132
  427.1 5.7 %multiply_reduce_fusion = f32[16,128]{0,1:T(8,128)S(1)} fusion(f32[16,16]{1,0:T(8,128)S(1)} %mul.242, bf16[16,16,16,128]{1,0,3,2:T(8,128)(2,1)} %bitcast.122), kind=kLoop, calls=%fused_computation.3 | loop fusion | flops 1570816 | bytes 1057792 | tf_op jit(solution)/shard_map/reduce_sum | solution.py:39
  432.9 11.5 %copy.66 = f32[16,16,16,128]{3,2,1,0:T(8,128)} copy(f32[16,16,16,128]{2,1,3,0:T(8,128)} %convert_bitcast_fusion.1) | data formatting | bytes 4194304 | tf_op jit(solution)/shard_map/convert_element_type | solution.py:132
  444.4 2.2 fusion.17
  446.6 3.6 fusion.20
  (53 shorter events, 1.7 us)
Async XLA Ops:
  7.2 181.3 %copy-start = (bf16[256,1024]{1,0:T(8,128)(2,1)S(1)}, bf16[256,1024]{1,0:T(8,128)(2,1)}, u32[]{:S(2)}) copy-start(bf16[256,1024]{1,0:T(8,128)(2,1)} %param.15) | copy-start | bytes 1572868
  7.2 3.2 copy-start.2
  7.2 3.2 copy-start.12
  7.2 98.9 %all-reduce.3.cloned.1.call-start = ((), (), s32[]{:S(2)}) async-start(), calls=%async_computation.4 | async-start | bytes 4194304 | tf_op jit(solution)/shard_map/psum | solution.py:57
  132.4 6.9 %copy-start.14 = (s32[16,128]{1,0:T(8,128)S(1)}, s32[16,128]{1,0:T(8,128)}, u32[]{:S(2)}) copy-start(s32[16,128]{1,0:T(8,128)} %param.18) | copy-start | bytes 24580
  132.4 7.0 %copy-start.16 = (s32[128]{0:T(128)S(1)}, s32[128]{0:T(128)}, u32[]{:S(2)}) copy-start(s32[128]{0:T(128)} %param.19) | copy-start | bytes 1540
  132.4 21.2 %all-to-all-start.1 = ((bf16[16,2,16384]{2,1,0:T(2,128)(2,1)}), bf16[16,2,16384]{2,1,0:T(2,128)(2,1)S(1)}, u32[]{:S(2)}, u32[]{:S(2)}) async-start(bf16[16,2,16384]{2,1,0:T(2,128)(2,1)} %reshape.152), calls=%async_computation.1 | async-start | bytes 2097152 | tf_op jit(solution)/shard_map/all_to_all | solution.py:49
  139.0 173.0 %all-reduce.5.cloned.1.call-start = ((), (), s32[]{:S(2)}) async-start(), calls=%async_computation.5 | async-start | bytes 4194304 | tf_op jit(solution)/shard_map/psum | solution.py:57
  187.4 0.7 copy-start.13
  188.5 1.6 copy-start.10
  188.5 1.7 copy-start.15
  189.8 3.3 copy-start.6
  190.1 3.0 copy-start.11
  193.2 1.0 copy-start.8
  211.7 2.2 copy-start.4
  211.7 2.9 copy-start.7
  339.7 6.8 %copy-start.9 = (bf16[256,2048]{0,1:T(8,128)(2,1)S(1)}, bf16[256,2048]{0,1:T(8,128)(2,1)}, u32[]{:S(2)}) copy-start(bf16[256,2048]{0,1:T(8,128)(2,1)} %copy-done.8) | copy-start | bytes 3145732
  339.7 69.0 %all-to-all-start.3 = ((bf16[16,2,16384]{2,1,0:T(2,128)(2,1)}), bf16[16,2,16384]{2,1,0:T(2,128)(2,1)S(1)}, u32[]{:S(2)}, u32[]{:S(2)}) async-start(bf16[16,2,16384]{2,1,0:T(2,128)(2,1)} %reshape.154), calls=%async_computation.3 | async-start | bytes 2097152 | tf_op jit(solution)/shard_map/all_to_all | solution.py:49
  432.9 11.5 %copy-start.3 = (bf16[256,16,128]{2,1,0:T(8,128)(2,1)S(1)}, bf16[256,16,128]{2,1,0:T(8,128)(2,1)}, u32[]{:S(2)}) copy-start(bf16[256,16,128]{2,1,0:T(8,128)(2,1)} %param.10) | copy-start | bytes 3145732
  444.4 2.2 copy-start.5
  446.6 3.6 copy-start.1
Sparse Core Ops, SparseCore 0:
  42.2 63.8 all-reduce.2
  241.5 70.5 all-reduce.4
